TPU v7x, 128 devices: a whole 4x4x4 slice. The times are simulated.
128 devices in a mesh: expert: 16 (over y, x), edata: 8 (over z, core).
Axes of the slice: x: 4, y: 4, z: 4, core: 2. Of those that a mesh axis runs over, the one named last changes fastest.
Arguments:
- out_grad: bfloat16 [131072, 4096], P(('expert', 'edata')), may hold values from -3.5 to 3.5
- hidden_saved: bfloat16 [131072, 768], P(('expert', 'edata')), may hold values from -6 to 6
- recv_counts: int32 [2048], P(('expert', 'edata')), may hold values from 1 to 64, as said below
- master_weight: float32 [65536, 768], P(('expert', 'edata'))
- moment_one: bfloat16 [65536, 768], P(('expert', 'edata')), may hold values from -4 to 4
- moment_two: bfloat16 [65536, 768], P(('expert', 'edata')), may hold values from 0.049804688 to 0.5
Outputs:
- new_master: float32 [65536, 768], P(('expert', 'edata'))
- new_moment_one: bfloat16 [65536, 768], P(('expert', 'edata'))
- new_moment_two: bfloat16 [65536, 768], P(('expert', 'edata'))
- scaled_weight: bfloat16 [65536, 768], P('expert')
- expert_peak: float32 [16], P('expert')
Inputs may be any that keep to these rules, and one draw needn't show every extreme that they name: `recv_counts`: counts are skewed over experts; in every draw some pair fills all 64 slots.
All inputs are finite; a program needn't handle non-finite values. Where the computation divides by a largest or mean magnitude, that divisor is 1e-20 or more.
Results may differ from a plain program's by a relative error of at most 0.001.
Values may be sent and summed in bfloat16 or wider, within the bound.
A program may use at most 128 MiB of HBM per device.

v0:
```python
import jax
import jax.numpy as jnp
from jax import lax
from jax.sharding import PartitionSpec as P

beta_one = 0.9
beta_two = 0.999
correct_one = 1.0 - 0.9**5
correct_two = 1.0 - 0.999**5
adam_eps = 1e-08
learn_rate = 0.05
weight_decay = 1.0
peak_eps = 1e-06


def local(out_grad, hidden_saved, recv_counts, master_weight, moment_one, moment_two):
    experts = lax.axis_size("expert")
    capacity = out_grad.shape[0] // experts
    arrived = lax.all_to_all(out_grad, "expert", split_axis=0, concat_axis=0, tiled=True)
    slots = jnp.arange(capacity)
    live = (slots[None, :] < recv_counts[:, None]).reshape(-1)
    masked = jnp.where(live[:, None], arrived, jnp.zeros((), jnp.bfloat16))
    grad = lax.psum_scatter(
        lax.dot_general(
            masked, hidden_saved, (((0,), (0,)), ((), ())), preferred_element_type=jnp.float32
        ),
        "edata",
        scatter_dimension=0,
        tiled=True,
    )
    first = beta_one * moment_one.astype(jnp.float32) + (1.0 - beta_one) * grad
    second = beta_two * moment_two.astype(jnp.float32) + (1.0 - beta_two) * grad * grad
    update = first / correct_one / (jnp.sqrt(second / correct_two) + adam_eps)
    new_master = master_weight - learn_rate * (update + weight_decay * master_weight)
    local_peak = jnp.max(jnp.abs(new_master))
    peak = lax.pmax(local_peak, "edata")
    scaled_shard = (new_master / (peak + peak_eps)).astype(jnp.bfloat16)
    scaled = lax.all_gather(scaled_shard, "edata", axis=0, tiled=True)
    return (
        new_master,
        first.astype(jnp.bfloat16),
        second.astype(jnp.bfloat16),
        scaled,
        peak.reshape(1),
    )


def solution(mesh):
    placed = (
        P(("expert", "edata"), None),
        P(("expert", "edata"), None),
        P(("expert", "edata")),
        P(("expert", "edata"), None),
        P(("expert", "edata"), None),
        P(("expert", "edata"), None),
    )
    return jax.shard_map(
        local,
        mesh=mesh,
        in_specs=placed,
        out_specs=(
            P(("expert", "edata"), None),
            P(("expert", "edata"), None),
            P(("expert", "edata"), None),
            P("expert", None),
            P("expert"),
        ),
        check_vma=False,
    )
```

profile of v0, /device:TPU:1, one launch (start us, length us, event | category | flops | bytes accessed | tf_op | source)
XLA Modules:
  0.0 306.5 jit_solution(4694745972800328352)
XLA Ops:
  7.2 0.0 copy-start
  7.2 0.0 copy-start.2
  7.2 7.8 %all-to-all-start = ((bf16[16,64,4096]{2,1,0:T(8,128)(2,1)}), bf16[16,64,4096]{2,1,0:T(8,128)(2,1)}, u32[]{:S(2)}, u32[]{:S(2)}) async-start(bf16[16,64,4096]{2,1,0:T(8,128)(2,1)} %bitcast.6), calls=%async_computation | async-start | bytes 16777216 | tf_op jit(solution)/shard_map/all_to_all | solution.py:19
  15.0 0.0 reduce-scatter.2.cloned.1.call-start
  15.0 0.0 copy-done.2
  15.0 0.1 iota_compare_fusion
  15.1 0.1 lt.23
  15.2 123.1 %all-to-all-done = bf16[16,64,4096]{2,1,0:T(8,128)(2,1)} async-done(((bf16[16,64,4096]{2,1,0:T(8,128)(2,1)}), bf16[16,64,4096]{2,1,0:T(8,128)(2,1)}, u32[]{:S(2)}, u32[]{:S(2)}) %all-to-all-start) | async-done | bytes 8388640 | tf_op jit(solution)/shard_map/all_to_all | solution.py:19
  138.3 7.2 %bitcast_select_fusion = bf16[1024,4096]{1,0:T(8,128)(2,1)} fusion(bf16[16,64,4096]{2,1,0:T(8,128)(2,1)} %all-to-all-done, pred[1024]{0:T(1024)(128)(4,1)S(1)} %lt.23), kind=kLoop, calls=%fused_computation | loop fusion | flops 4194304 | bytes 16778240 | tf_op jit(solution)/shard_map/jit(_where)/select_n | solution.py:22
  145.5 0.0 copy-done
  145.5 12.9 %fusion.3 = f32[4096,768]{1,0:T(8,128)} fusion(bf16[1024,4096]{1,0:T(8,128)(2,1)} %bitcast_select_fusion, bf16[1024,768]{1,0:T(8,128)(2,1)S(1)} %copy-done), kind=kOutput, calls=%fused_computation.10 | convolution fusion | flops 6442450944 | bytes 22544384 | tf_op jit(solution)/shard_map/dot_general | solution.py:24
  158.4 0.0 reduce-scatter.2.cloned.1.call-update
  158.4 0.0 all-gather.2.cloned.1.call-start
  158.5 74.1 %reduce-scatter.2.cloned.1.call-done = f32[512,768]{1,0:T(8,128)} async-done(((f32[4096,768]{1,0:T(8,128)}), f32[512,768]{1,0:T(8,128)}) %reduce-scatter.2.cloned.1.call-update) | async-done | bytes 1572880 | tf_op jit(solution)/shard_map/reduce_scatter | solution.py:23
  232.5 5.4 %abs_reduce_fusion = (f32[]{:T(128)}, f32[512,768]{1,0:T(8,128)S(1)}, bf16[512,768]{1,0:T(8,128)(2,1)}, bf16[512,768]{1,0:T(8,128)(2,1)}) fusion(f32[512,768]{1,0:T(8,128)} %param.9, f32[512,768]{1,0:T(8,128)} %reduce-scatter.2.cloned.1.call-done, bf16[512,768]{1,0:T(8,128)(2,1)} %param.11, bf16[512,768]{1,0:T(8,128)(2,1)} %param.10), kind=kLoop, calls=%fused_computation.4 | loop fusion | flops 7864319 | bytes 7864324 | tf_op jit(solution)/shard_map/reduce_max | solution.py:35
  238.0 0.0 copy-start.1
  238.0 13.8 %pmax.7 = f32[]{:T(128)} all-reduce(f32[]{:T(128)} %get-tuple-element.5), channel_id=1, replica_groups=mesh['expert'=16,'edata'=8] {'edata'}, use_global_device_ids=true, to_apply=%region_2.3 | all-reduce | flops 1 | bytes 8 | tf_op jit(solution)/shard_map/pmax | solution.py:36
  252.4 1.0 divide_convert_fusion
  253.4 0.0 all-gather.2.cloned.1.call-update
  253.4 0.0 copy-done.1
  253.4 40.4 %all-gather.2.cloned.1.call-done = bf16[4096,768]{1,0:T(8,128)(2,1)} async-done(((bf16[512,768]{1,0:T(8,128)(2,1)}), bf16[4096,768]{1,0:T(8,128)(2,1)}) %all-gather.2.cloned.1.call-update) | async-done | bytes 6291472 | tf_op jit(solution)/shard_map/all_gather | solution.py:38
  293.8 5.9 %copy.12 = bf16[4096,768]{1,0:T(8,128)(2,1)} copy(bf16[4096,768]{1,0:T(8,128)(2,1)} %all-gather.2.cloned.1.call-done) | data formatting | bytes 12582912
Async XLA Ops:
  7.2 138.4 %copy-start = (bf16[1024,768]{1,0:T(8,128)(2,1)S(1)}, bf16[1024,768]{1,0:T(8,128)(2,1)}, u32[]{:S(2)}) copy-start(bf16[1024,768]{1,0:T(8,128)(2,1)} %param.7) | copy-start | bytes 4718596
  7.2 7.8 %copy-start.2 = (s32[16]{0:T(128)S(1)}, s32[16]{0:T(128)}, u32[]{:S(2)}) copy-start(s32[16]{0:T(128)} %param.8) | copy-start | bytes 196
  7.2 131.1 %all-to-all-start = ((bf16[16,64,4096]{2,1,0:T(8,128)(2,1)}), bf16[16,64,4096]{2,1,0:T(8,128)(2,1)}, u32[]{:S(2)}, u32[]{:S(2)}) async-start(bf16[16,64,4096]{2,1,0:T(8,128)(2,1)} %bitcast.6), calls=%async_computation | async-start | bytes 16777216 | tf_op jit(solution)/shard_map/all_to_all | solution.py:19
  15.0 217.6 %reduce-scatter.2.cloned.1.call-start = ((), (), s32[]{:S(2)}) async-start(), calls=%async_computation.2 | async-start | bytes 14155776 | tf_op jit(solution)/shard_map/reduce_scatter | solution.py:23
  158.4 135.4 %all-gather.2.cloned.1.call-start = ((), (), s32[]{:S(2)}) async-start(), calls=%async_computation.3 | async-start | bytes 7077888 | tf_op jit(solution)/shard_map/all_gather | solution.py:38
  238.0 15.4 %copy-start.1 = (f32[512,768]{1,0:T(8,128)}, f32[512,768]{1,0:T(8,128)S(1)}, u32[]{:S(2)}) copy-start(f32[512,768]{1,0:T(8,128)S(1)} %get-tuple-element.14) | copy-start | bytes 4718596
Sparse Core Ops, SparseCore 0:
  158.5 73.9 reduce-scatter.1
  253.5 40.2 all-gather.1
where the time goes:
time: 307 us
  waiting for transfers between devices  238 us (78%)
  between operations  14.7 us (5%)
  blocking collectives  13.8 us (4%)
  other arithmetic  13.7 us (4%)
  matrix products  12.9 us (4%)
  starting transfers between devices  7.85 us (3%)
  local copies, waits for them, and re-layouts  6 us (2%)
    all_to_all x1, waiting for transfers between devices, local(): lax.all_to_all(out_grad, 'expert', split_axis=0, concat_axis=0, tiled=True)  123 us
    reduce_scatter x1, waiting for transfers between devices, local(): lax.psum_scatter(lax.dot_general(masked, hidden_saved, (((0,), (0,)), (()...  74.1 us
    all_gather x1, waiting for transfers between devices, local(): scaled = lax.all_gather(scaled_shard, 'edata', axis=0, tiled=True)  40.4 us
    pmax x1, blocking collectives, local(): peak = lax.pmax(local_peak, 'edata')  13.8 us
    dot_general x1, matrix products, local(): lax.dot_general(masked, hidden_saved, (((0,), (0,)), ((), ())), preferred...  12.9 us
    all_to_all x1, starting transfers between devices, local(): lax.all_to_all(out_grad, 'expert', split_axis=0, concat_axis=0, tiled=True)  7.77 us
    select_n x1, other arithmetic, local(): masked = jnp.where(live[:, None], arrived, jnp.zeros((), jnp.bfloat16))  7.22 us
  transfers between devices with their start and end apart: 3, of which 3 were waited for; matrix products, arithmetic and copies ran while one was open for 0% of the time, Pallas kernels for 0%

commit v1 on v0

v1 whole, which is shorter than its diff:
```python
import functools

import jax
import jax.numpy as jnp
from jax import lax
from jax.experimental import pallas as pl
from jax.experimental.pallas import tpu as pltpu
from jax.sharding import PartitionSpec as P

MESH = pl.DeviceIdType.MESH

beta_one = 0.9
beta_two = 0.999
correct_one = 1.0 - 0.9**5
correct_two = 1.0 - 0.999**5
adam_eps = 1e-08
learn_rate = 0.05
weight_decay = 1.0
peak_eps = 1e-06

D = 4096
FFN = 768
HALF = FFN // 2
NC = 8
AHEAD = 3


def exchange_kernel(
    x_ref, h_ref, cnt_ref, mw_ref, m1_ref, m2_ref,
    w_ref, m1o_ref, m2o_ref,
    F, RA, RB, H, HT, PB, DB, ZR, ZF, mw, m1, m2, nm, n1, n2,
    l1, s1, r1, s2, r2, l2, ds, dr, zs, zr, gs, gr, ls, isem,
):
    e = lax.axis_index("expert")
    k = lax.axis_index("edata")
    y, x = e // 4, lax.rem(e, 4)
    z, c = k // 2, lax.rem(k, 2)
    zp, zm, zo = lax.rem(z + 1, 4), lax.rem(z + 3, 4), lax.rem(z + 2, 4)
    sib = (e, 2 * z + 1 - c)
    up = (e, 2 * zp + c)
    down = (e, 2 * zm + c)
    hops = (1, 3, 2)

    def xdev(p):
        return (y * 4 + p, k)

    def ydev(p):
        return (p * 4 + x, k)

    def rc(src, dst, ssem, rsem, dev):
        return pltpu.make_async_remote_copy(
            src_ref=src, dst_ref=dst, send_sem=ssem, recv_sem=rsem,
            device_id=dev, device_id_type=MESH,
        )

    lc = pltpu.make_async_copy

    barrier = pltpu.get_barrier_semaphore()
    for d in hops:
        pl.semaphore_signal(barrier, inc=1, device_id=xdev(lax.rem(x + d, 4)), device_id_type=MESH)
        pl.semaphore_signal(barrier, inc=1, device_id=ydev(lax.rem(y + d, 4)), device_id_type=MESH)
    for dev in (sib, up, down):
        pl.semaphore_signal(barrier, inc=1, device_id=dev, device_id_type=MESH)

    ins = (
        lc(h_ref, H, isem.at[0]),
        lc(mw_ref, mw, isem.at[1]),
        lc(m1_ref, m1, isem.at[2]),
        lc(m2_ref, m2, isem.at[3]),
    )
    for cp in ins:
        cp.start()
    pl.semaphore_wait(barrier, 9)

    R = (RA, RB)
    own1 = (x, y)
    own2 = (y, x)

    def start1(j):
        base = 512 * lax.rem(j, 2) + 128 * (j // 2)

        def src(h, p, s):
            cols = pl.ds(pl.multiple_of(1024 * s + base, 128), 128)
            if h == 0:
                return x_ref.at[:, p, pl.ds(0, 32), cols]
            return x_ref.at[p, :, pl.ds(32, 32), cols]

        for i, d in enumerate(hops):
            for h in (0, 1):
                p = lax.rem(own1[h] + d, 4)
                for s in range(4):
                    rc(
                        src(h, p, s), R[h].at[j, :, own1[h], :, pl.ds(128 * s, 128)],
                        s1.at[h, j, i], r1.at[h, j, i], (xdev, ydev)[h](p),
                    ).start()
        for h in (0, 1):
            for s in range(4):
                lc(src(h, own1[h], s), R[h].at[j, :, own1[h], :, pl.ds(128 * s, 128)], l1.at[h, j]).start()

    def dst2(h, j):
        if h == 0:
            return F.at[j, y, :, pl.ds(0, 32)]
        return F.at[j, :, x, pl.ds(32, 32)]

    def start2(j):
        for h in (0, 1):
            mine = R[h].at[j, :, own1[h]]
            lc(mine, mine, l1.at[h, j]).wait()
            for i, d in enumerate(hops):
                got = R[h].at[j, :, lax.rem(own1[h] + 4 - d, 4)]
                rc(got, got, s1.at[h, j, i], r1.at[h, j, i], sib).wait_recv()
            for i, d in enumerate(hops):
                p = lax.rem(own2[h] + d, 4)
                rc(R[h].at[j, p], dst2(h, j), s2.at[h, j, i], r2.at[h, j, i], (ydev, xdev)[h](p)).start()
            lc(R[h].at[j, own2[h]], dst2(h, j), l2.at[h, j]).start()

    def got2(h, j, i):
        p = lax.rem(own2[h] + 4 - hops[i], 4)
        if h == 0:
            return F.at[j, p, :, pl.ds(0, 32)]
        return F.at[j, :, p, pl.ds(32, 32)]

    def multiply(j):
        for h in (0, 1):
            for i in range(3):
                g = got2(h, j, i)
                rc(g, g, s2.at[h, j, i], r2.at[h, j, i], sib).wait_recv()
            lc(R[h].at[j, own2[h]], dst2(h, j), l2.at[h, j]).wait()
        for n in range(2):
            a = F[j, :, :, :, pl.ds(256 * n, 256)].reshape(1024, 256)
            prod = jnp.dot(HT[...], a, preferred_element_type=jnp.float32)
            PB[j, 2 * n] = prod[:, :128]
            PB[j, 2 * n + 1] = prod[:, 128:]

    def to_sibling(j):
        return rc(PB.at[j], DB.at[j // 2], ds.at[j // 2], dr.at[j // 2], sib)

    def zcopies(j):
        q = j // 2
        lo, hi = pl.ds(0, HALF), pl.ds(HALF, HALF)
        return (
            rc(PB.at[j, zo, lo], ZR.at[q, 0], zs.at[q, 0], zr.at[q, 0], up),
            rc(PB.at[j, zo, hi], ZR.at[q, 1], zs.at[q, 1], zr.at[q, 1], down),
            rc(PB.at[j, zp, hi], ZF.at[q, 0, hi], zs.at[q, 2], zr.at[q, 2], up),
            rc(PB.at[j, zm, lo], ZF.at[q, 1, lo], zs.at[q, 3], zr.at[q, 3], down),
            rc(PB.at[j, zp, lo], ZF.at[q, 0, lo], zs.at[q, 4], zr.at[q, 4], up),
            rc(PB.at[j, zm, hi], ZF.at[q, 1, hi], zs.at[q, 5], zr.at[q, 5], down),
        )

    def reduce_one(j):
        q = j // 2
        to_sibling(j).wait_recv()
        cps = zcopies(j)
        PB[j, zo] = PB[j, zo] + DB[q, zo]
        cps[0].start()
        cps[1].start()
        PB[j, zp] = PB[j, zp] + DB[q, zp]
        cps[2].start()
        PB[j, zm] = PB[j, zm] + DB[q, zm]
        cps[3].start()
        PB[j, z] = PB[j, z] + DB[q, z]

    def reduce_two(j):
        q = j // 2
        cps = zcopies(j)
        cps[0].wait_recv()
        PB[j, zp, pl.ds(0, HALF)] = PB[j, zp, pl.ds(0, HALF)] + ZR[q, 0]
        cps[4].start()
        cps[1].wait_recv()
        PB[j, zm, pl.ds(HALF, HALF)] = PB[j, zm, pl.ds(HALF, HALF)] + ZR[q, 1]
        cps[5].start()

    def block(zz, q, first=0, rows=128):
        start = (2 * zz + c) * 512 + 128 * q + first
        return w_ref.at[pl.ds(pl.multiple_of(start, 64), rows)]

    def gcopies(q):
        own = nm.at[pl.ds(pl.multiple_of(128 * q, 128), 128)]
        return (
            rc(own, block(z, q), gs.at[q, 0], gr.at[q, 0], up),
            rc(own, block(z, q), gs.at[q, 1], gr.at[q, 1], down),
            rc(own, block(z, q), gs.at[q, 4], gr.at[q, 4], sib),
        )

    def lcopies(q):
        rows = pl.ds(pl.multiple_of(128 * q, 128), 128)
        return (
            lc(nm.at[rows], block(z, q), ls.at[q, 0]),
            lc(n1.at[rows], m1o_ref.at[rows], ls.at[q, 1]),
            lc(n2.at[rows], m2o_ref.at[rows], ls.at[q, 2]),
        )

    def finish(j):
        q = j // 2
        cps = zcopies(j)
        cps[2].wait_recv()
        cps[3].wait_recv()
        cps[4].wait_recv()
        cps[5].wait_recv()
        grad = (PB[j, z] + ZF[q, 0] + ZF[q, 1]).T
        rows = pl.ds(pl.multiple_of(128 * q, 128), 128)
        first = beta_one * m1[rows].astype(jnp.float32) + (1.0 - beta_one) * grad
        second = beta_two * m2[rows].astype(jnp.float32) + (1.0 - beta_two) * grad * grad
        update = first / correct_one / (jnp.sqrt(second / correct_two) + adam_eps)
        weight = mw[rows]
        nm[rows] = weight - learn_rate * (update + weight_decay * weight)
        n1[rows] = first.astype(jnp.bfloat16)
        n2[rows] = second.astype(jnp.bfloat16)
        for cp in gcopies(q) + lcopies(q):
            cp.start()

    def fcopies(q):
        return (
            rc(block(zm, q, 0, 64), block(zm, q, 0, 64), gs.at[q, 2], gr.at[q, 2], up),
            rc(block(zp, q, 64, 64), block(zp, q, 64, 64), gs.at[q, 3], gr.at[q, 3], down),
            rc(block(zm, q), block(zm, q), gs.at[q, 5], gr.at[q, 5], sib),
            rc(block(zp, q), block(zp, q), gs.at[q, 6], gr.at[q, 6], sib),
            rc(block(zo, q), block(zo, q), gs.at[q, 7], gr.at[q, 7], sib),
        )

    def forward_one(j):
        q = j // 2
        g, f = gcopies(q), fcopies(q)
        g[0].wait_recv()
        f[0].start()
        f[2].start()
        g[1].wait_recv()
        f[1].start()
        f[3].start()

    def forward_two(j):
        f = fcopies(j // 2)
        f[0].wait_recv()
        f[1].wait_recv()
        f[4].start()

    for j in range(AHEAD):
        start1(j)

    ins[0].wait()
    slot = lax.broadcasted_iota(jnp.int32, (64, FFN), 0)
    for s in range(8):
        parts = []
        for t in (2 * s, 2 * s + 1):
            rows = H[pl.ds(64 * t, 64)].astype(jnp.float32)
            parts.append(jnp.where(slot < cnt_ref[t], rows, 0.0))
        HT[:, pl.ds(128 * s, 128)] = jnp.concatenate(parts, axis=0).T.astype(jnp.bfloat16)
    for cp in ins[1:]:
        cp.wait()

    def step(t, carry):
        @pl.when(t < NC)
        def _():
            start2(t)

        @pl.when(t + AHEAD < NC)
        def _():
            start1(t + AHEAD)

        def stage(lag, fn):
            j = t - lag

            @pl.when((j >= 0) & (j < NC) & (lax.rem(j + 2 * NC, 2) == c))
            def _():
                fn(j)

        stage(4, forward_two)
        stage(3, forward_one)

        j = t - 1

        @pl.when((j >= 0) & (j < NC))
        def _():
            multiply(j)

            @pl.when(lax.rem(j, 2) != c)
            def _():
                to_sibling(j).start()

        stage(1, reduce_one)
        stage(2, reduce_two)
        stage(2, finish)
        return carry

    lax.fori_loop(0, NC + 4, step, 0)

    def drain(q, carry):
        f = fcopies(q)
        blocks = (z, zm, zp, zo)
        for i in range(4):
            start = (2 * blocks[i] + 1 - c) * 512 + 128 * q
            b = w_ref.at[pl.ds(pl.multiple_of(start, 128), 128)]
            rc(b, b, gs.at[q, 4 + i], gr.at[q, 4 + i], sib).wait_recv()
        for cp in gcopies(q) + f:
            cp.wait_send()
        for cp in lcopies(q):
            cp.wait()
        for cp in zcopies(2 * q + c):
            cp.wait_send()
        to_sibling(2 * q + 1 - c).wait_send()
        return carry

    lax.fori_loop(0, NC // 2, drain, 0)

    def drain_sends(j, carry):
        for h in (0, 1):
            for i in range(3):
                a = R[h].at[j, :, 0]
                rc(a, a, s1.at[h, j, i], r1.at[h, j, i], sib).wait_send()
                a = R[h].at[j, 0]
                rc(a, a, s2.at[h, j, i], r2.at[h, j, i], sib).wait_send()
        return carry

    lax.fori_loop(0, NC, drain_sends, 0)


def exchange(out_grad, hidden, counts, master, m1, m2):
    V, DMA = pltpu.VMEM, pltpu.SemaphoreType.DMA
    f32, bf16 = jnp.float32, jnp.bfloat16
    any_spec = pl.BlockSpec(memory_space=pl.ANY)
    rows = master.shape[0]
    return pl.pallas_call(
        exchange_kernel,
        name="exchange",
        out_shape=(
            jax.ShapeDtypeStruct((D, FFN), f32),
            jax.ShapeDtypeStruct((rows, FFN), bf16),
            jax.ShapeDtypeStruct((rows, FFN), bf16),
        ),
        in_specs=[any_spec, any_spec, pl.BlockSpec(memory_space=pltpu.SMEM), any_spec, any_spec, any_spec],
        out_specs=(any_spec, any_spec, any_spec),
        scratch_shapes=[
            V((NC, 4, 4, 64, 512), bf16),
            V((NC, 4, 4, 32, 512), bf16),
            V((NC, 4, 4, 32, 512), bf16),
            V((1024, FFN), bf16),
            V((FFN, 1024), bf16),
            V((NC, 4, FFN, 128), f32),
            V((NC // 2, 4, FFN, 128), f32),
            V((NC // 2, 2, HALF, 128), f32),
            V((NC // 2, 2, FFN, 128), f32),
            V((rows, FFN), f32),
            V((rows, FFN), bf16),
            V((rows, FFN), bf16),
            V((rows, FFN), f32),
            V((rows, FFN), bf16),
            V((rows, FFN), bf16),
            DMA((2, NC)),
            DMA((2, NC, 3)),
            DMA((2, NC, 3)),
            DMA((2, NC, 3)),
            DMA((2, NC, 3)),
            DMA((2, NC)),
            DMA((NC // 2,)),
            DMA((NC // 2,)),
            DMA((NC // 2, 6)),
            DMA((NC // 2, 6)),
            DMA((NC // 2, 8)),
            DMA((NC // 2, 8)),
            DMA((NC // 2, 3)),
            DMA((4,)),
        ],
        compiler_params=pltpu.CompilerParams(
            collective_id=0, has_side_effects=True, vmem_limit_bytes=62 << 20
        ),
    )(out_grad.reshape(4, 4, 64, D), hidden, counts, master, m1, m2)


BLOCKS = 8
ROWS = D // BLOCKS


def scale_kernel(w_ref, m1_ref, m2_ref, nm_ref, m1o_ref, m2o_ref, s_ref, peak_ref, wv, sv, v1, v2, isem, osem):
    k = lax.axis_index("edata")
    lc = pltpu.make_async_copy

    def load(b):
        return lc(w_ref.at[pl.ds(b * ROWS, ROWS)], wv.at[b], isem.at[b])

    for b in range(BLOCKS):
        load(b).start()
    small = (lc(m1_ref, v1, isem.at[BLOCKS]), lc(m2_ref, v2, isem.at[BLOCKS + 1]))
    for cp in small:
        cp.start()
    top = jnp.zeros((64, FFN), jnp.float32)
    for b in range(BLOCKS):
        load(b).wait()

        def biggest(i, best, b=b):
            return jnp.maximum(best, jnp.abs(wv[b, pl.ds(pl.multiple_of(64 * i, 64), 64)]))

        top = lax.fori_loop(0, ROWS // 64, biggest, top)
    outs = [lc(wv.at[k], nm_ref, osem.at[BLOCKS])]
    outs[0].start()
    for cp, v, o, i in ((small[0], v1, m1o_ref, 1), (small[1], v2, m2o_ref, 2)):
        cp.wait()
        outs.append(lc(v, o, osem.at[BLOCKS + i]))
        outs[-1].start()
    peak = jnp.max(top)
    peak_ref[0] = peak
    whole = jnp.full((8, FFN), peak + peak_eps, jnp.float32)
    shrink = jnp.where(whole > 2.0**100, jnp.float32(2.0**-64), jnp.float32(1.0))
    factor = 1.0 / (whole * shrink)
    for b in range(BLOCKS):
        def put(i, carry, b=b):
            rows = pl.ds(pl.multiple_of(64 * i, 64), 64)
            v = wv[b, rows].reshape(8, 8, FFN)
            sv[b, rows] = ((v * shrink) * factor).reshape(64, FFN).astype(jnp.bfloat16)
            return carry

        lax.fori_loop(0, ROWS // 64, put, 0)
        outs.append(lc(sv.at[b], s_ref.at[pl.ds(b * ROWS, ROWS)], osem.at[b]))
        outs[-1].start()
    for cp in outs:
        cp.wait()


def scale(w, m1, m2):
    V, DMA = pltpu.VMEM, pltpu.SemaphoreType.DMA
    f32, bf16 = jnp.float32, jnp.bfloat16
    any_spec = pl.BlockSpec(memory_space=pl.ANY)
    rows = m1.shape[0]
    return pl.pallas_call(
        scale_kernel,
        name="scale",
        out_shape=(
            jax.ShapeDtypeStruct((rows, FFN), f32),
            jax.ShapeDtypeStruct((rows, FFN), bf16),
            jax.ShapeDtypeStruct((rows, FFN), bf16),
            jax.ShapeDtypeStruct((D, FFN), bf16),
            jax.ShapeDtypeStruct((1,), f32),
        ),
        in_specs=[any_spec] * 3,
        out_specs=(any_spec,) * 4 + (pl.BlockSpec(memory_space=pltpu.SMEM),),
        scratch_shapes=[
            V((BLOCKS, ROWS, FFN), f32),
            V((BLOCKS, ROWS, FFN), bf16),
            V((rows, FFN), bf16),
            V((rows, FFN), bf16),
            DMA((BLOCKS + 2,)),
            DMA((BLOCKS + 3,)),
        ],
        compiler_params=pltpu.CompilerParams(vmem_limit_bytes=40 << 20),
    )(w, m1, m2)


def local(out_grad, hidden_saved, recv_counts, master_weight, moment_one, moment_two):
    w, n1, n2 = exchange(out_grad, hidden_saved, recv_counts, master_weight, moment_one, moment_two)
    new_master, n1, n2, scaled, peak = scale(w, n1, n2)
    return new_master, n1, n2, scaled, peak


def solution(mesh):
    placed = (
        P(("expert", "edata"), None),
        P(("expert", "edata"), None),
        P(("expert", "edata")),
        P(("expert", "edata"), None),
        P(("expert", "edata"), None),
        P(("expert", "edata"), None),
    )
    return jax.shard_map(
        local,
        mesh=mesh,
        in_specs=placed,
        out_specs=(
            P(("expert", "edata"), None),
            P(("expert", "edata"), None),
            P(("expert", "edata"), None),
            P("expert", None),
            P("expert"),
        ),
        check_vma=False,
    )
```

time: 307 us -> 174 us (0.57)
  waiting for transfers between devices: 238 us -> 0 us
  Pallas kernels: 0 us -> 166 us
  between operations: 14.7 us -> 0.65 us
  blocking collectives: 13.8 us -> 0 us
  other arithmetic: 13.7 us -> 0 us
  matrix products: 12.9 us -> 0 us
  starting transfers between devices: 7.85 us -> 0 us
    pallas_call x0 -> x2, Pallas kernels: none -> 166 us  [the longest x1 159 us: exchange(): pl.pallas_call(exchange_kernel, name='exchange', out_shape=(jax.ShapeDtyp...]
    all_to_all x1 -> x0, waiting for transfers between devices: 123 us -> none  [local(): lax.all_to_all(out_grad, 'expert', split_axis=0, concat_axis=0, tiled=True)]
    reduce_scatter x1 -> x0, waiting for transfers between devices: 74.1 us -> none  [local(): lax.psum_scatter(lax.dot_general(masked, hidden_saved, (((0,), (0,)), (()...]
    all_gather x1 -> x0, waiting for transfers between devices: 40.4 us -> none  [local(): scaled = lax.all_gather(scaled_shard, 'edata', axis=0, tiled=True)]
    pmax x1 -> x0, blocking collectives: 13.8 us -> none  [local(): peak = lax.pmax(local_peak, 'edata')]
    dot_general x1 -> x0, matrix products: 12.9 us -> none  [local(): lax.dot_general(masked, hidden_saved, (((0,), (0,)), ((), ())), preferred...]
    all_to_all x1 -> x0, starting transfers between devices: 7.77 us -> none  [local(): lax.all_to_all(out_grad, 'expert', split_axis=0, concat_axis=0, tiled=True)]
    select_n x1 -> x0, other arithmetic: 7.22 us -> none  [local(): masked = jnp.where(live[:, None], arrived, jnp.zeros((), jnp.bfloat16))]
  transfers between devices with their start and end apart: 3 -> 0, of which waited for: 3 -> 0; matrix products, arithmetic and copies ran while one was open for 0% -> 0% of each run, Pallas kernels for 0% -> 0%
where the time goes in v1:
time: 174 us
  Pallas kernels  166 us (95%)
  local copies, waits for them, and re-layouts  6.83 us (4%)
    pallas_call x1, Pallas kernels, exchange(): pl.pallas_call(exchange_kernel, name='exchange', out_shape=(jax.ShapeDtyp...  159 us
    pallas_call x1, Pallas kernels, scale(): pl.pallas_call(scale_kernel, name='scale', out_shape=(jax.ShapeDtypeStruc...  7.41 us
    unnamed x6, local copies, waits for them, and re-layouts  6.83 us

profile of v1, /device:TPU:1, one launch (start us, length us, event | category | flops | bytes accessed | tf_op | source)
XLA Modules:
  0.0 174.0 jit_solution(6084445295452328208)
XLA Ops:
  0.6 159.1 %exchange.1 = (f32[4096,768]{1,0:T(8,128)}, bf16[512,768]{1,0:T(8,128)(2,1)}, bf16[512,768]{1,0:T(8,128)(2,1)}) custom-call(bf16[4,4,64,4096]{3,2,1,0:T(8,128)(2,1)} %bitcast.1, bf16[1024,768]{1,0:T(8,128)(2,1)} %h_ref.1, s32[16]{0:T(128)} %cnt_ref.1, f32[512,768]{1,0:T(8,128)} %mw_ref.1, bf16[512,768]{1,0:T(8,128)(2,1)} %m1_ref.1, bf16[512,768]{1,0:T(8,128)(2,1)} %m2_ref.1), custom_call_target="tpu_custom_call" | custom-call | tf_op jit(solution)/shard_map/exchange/pallas_call | solution.py:322
  159.7 0.0 copy-start
  159.7 4.6 %copy-done = f32[4096,768]{1,0:T(8,128)S(1)} copy-done((f32[4096,768]{1,0:T(8,128)S(1)}, f32[4096,768]{1,0:T(8,128)}, u32[]{:S(2)}) %copy-start) | copy-done | bytes 12582936
  164.3 0.0 copy-start.1
  164.3 1.1 copy-done.1
  165.4 0.0 copy-start.2
  165.4 1.1 copy-done.2
  166.5 7.4 %scale.1 = (f32[512,768]{1,0:T(8,128)}, bf16[512,768]{1,0:T(8,128)(2,1)}, bf16[512,768]{1,0:T(8,128)(2,1)}, bf16[4096,768]{1,0:T(8,128)(2,1)}, f32[1]{0:T(128)}) custom-call(f32[4096,768]{1,0:T(8,128)S(1)} %copy-done, bf16[512,768]{1,0:T(8,128)(2,1)S(1)} %copy-done.1, bf16[512,768]{1,0:T(8,128)(2,1)S(1)} %copy-done.2), custom_call_target="tpu_custom_call" | custom-call | tf_op jit(solution)/shard_map/scale/pallas_call | solution.py:423
Async XLA Ops:
  159.7 4.6 %copy-start = (f32[4096,768]{1,0:T(8,128)S(1)}, f32[4096,768]{1,0:T(8,128)}, u32[]{:S(2)}) copy-start(f32[4096,768]{1,0:T(8,128)} %get-tuple-element.8.w_ref) | copy-start | bytes 37748740
  164.3 1.1 copy-start.1
  165.4 1.1 copy-start.2

commit v2 on v1

--- a/solution.py
+++ b/solution.py
@@ -22,14 +22,28 @@
 FFN = 768
 HALF = FFN // 2
 NC = 8
-AHEAD = 3
+AHEAD = 2
+QN = NC // 2
+EARLY = 96
+EARLY_LAST = 48
+LATE = 128 - EARLY
+EN = (QN - 1) * EARLY + EARLY_LAST
+LN = 128 * QN - EN
+LA = (QN - 1) * LATE
+LB = 128 - EARLY_LAST
+
+
+def scale_factors(peak, rows):
+    whole = jnp.full((rows, FFN), peak + peak_eps, jnp.float32)
+    shrink = jnp.where(whole > 2.0**100, jnp.float32(2.0**-64), jnp.float32(1.0))
+    return shrink, 1.0 / (whole * shrink)
 
 
 def exchange_kernel(
     x_ref, h_ref, cnt_ref, mw_ref, m1_ref, m2_ref,
-    w_ref, m1o_ref, m2o_ref,
-    F, RA, RB, H, HT, PB, DB, ZR, ZF, mw, m1, m2, nm, n1, n2,
-    l1, s1, r1, s2, r2, l2, ds, dr, zs, zr, gs, gr, ls, isem,
+    w_ref, sl_ref, nmo_ref, m1o_ref, m2o_ref, pk_ref,
+    F, RA, RB, H, HT, PB, DB, ZR, ZF, mw, m1, m2, nm, n1, n2, sl, PK, top,
+    l1, s1, r1, s2, r2, l2, ds, dr, zs, zr, gs, gr, gl, ls, isem, ps, pr,
 ):
     e = lax.axis_index("expert")
     k = lax.axis_index("edata")
@@ -59,7 +73,8 @@
     for d in hops:
         pl.semaphore_signal(barrier, inc=1, device_id=xdev(lax.rem(x + d, 4)), device_id_type=MESH)
         pl.semaphore_signal(barrier, inc=1, device_id=ydev(lax.rem(y + d, 4)), device_id_type=MESH)
-    for dev in (sib, up, down):
+    for i in range(1, 8):
+        dev = (e, lax.rem(k + i, 8))
         pl.semaphore_signal(barrier, inc=1, device_id=dev, device_id_type=MESH)
 
     ins = (
@@ -70,7 +85,7 @@
     )
     for cp in ins:
         cp.start()
-    pl.semaphore_wait(barrier, 9)
+    pl.semaphore_wait(barrier, 13)
 
     R = (RA, RB)
     own1 = (x, y)
@@ -170,22 +185,40 @@
         PB[j, zm, pl.ds(HALF, HALF)] = PB[j, zm, pl.ds(HALF, HALF)] + ZR[q, 1]
         cps[5].start()
 
-    def block(zz, q, first=0, rows=128):
-        start = (2 * zz + c) * 512 + 128 * q + first
-        return w_ref.at[pl.ds(pl.multiple_of(start, 64), rows)]
-
-    def gcopies(q):
-        own = nm.at[pl.ds(pl.multiple_of(128 * q, 128), 128)]
+    def rows_of(q):
+        return pl.ds(pl.multiple_of(128 * q, 128), 128)
+
+    def part(g, last):
+        if last is None:
+            return w_ref, pl.multiple_of(EARLY * g, 8), EARLY, EARLY // 2
         return (
-            rc(own, block(z, q), gs.at[q, 0], gr.at[q, 0], up),
-            rc(own, block(z, q), gs.at[q, 1], gr.at[q, 1], down),
-            rc(own, block(z, q), gs.at[q, 4], gr.at[q, 4], sib),
+            (w_ref, (QN - 1) * EARLY, EARLY_LAST, EARLY_LAST // 2),
+            (sl_ref, 0, LA, LA // 32 * 16),
+            (sl_ref, LA, LB, (LB + 31) // 32 * 16),
+        )[last]
+
+    def block(kk, g, last, piece=0):
+        ref, off, n, cut = part(g, last)
+        first, count = ((0, n), (0, cut), (cut, n - cut))[piece]
+        return ref.at[kk, pl.ds(off + first, count)]
+
+    def gcopies(g, last=None):
+        if last is None:
+            own = nm.at[pl.ds(pl.multiple_of(128 * g, 128), EARLY)]
+        else:
+            own = (nm.at[pl.ds(128 * (QN - 1), EARLY_LAST)], sl.at[pl.ds(0, LA)], sl.at[pl.ds(LA, LB)])[last]
+        b = block(k, g, last)
+        return (
+            rc(own, b, gs.at[g, 0], gr.at[g, 0], up),
+            rc(own, b, gs.at[g, 1], gr.at[g, 1], down),
+            rc(own, b, gs.at[g, 4], gr.at[g, 4], sib),
+            lc(own, b, gl.at[g]),
         )
 
     def lcopies(q):
-        rows = pl.ds(pl.multiple_of(128 * q, 128), 128)
+        rows = rows_of(q)
         return (
-            lc(nm.at[rows], block(z, q), ls.at[q, 0]),
+            lc(nm.at[rows], nmo_ref.at[rows], ls.at[q, 0]),
             lc(n1.at[rows], m1o_ref.at[rows], ls.at[q, 1]),
             lc(n2.at[rows], m2o_ref.at[rows], ls.at[q, 2]),
         )
@@ -203,39 +236,56 @@
         second = beta_two * m2[rows].astype(jnp.float32) + (1.0 - beta_two) * grad * grad
         update = first / correct_one / (jnp.sqrt(second / correct_two) + adam_eps)
         weight = mw[rows]
-        nm[rows] = weight - learn_rate * (update + weight_decay * weight)
+        weight = weight - learn_rate * (update + weight_decay * weight)
+        nm[rows] = weight
+        size = jnp.abs(weight)
+        most = size[:8]
+        for i in range(1, 16):
+            most = jnp.maximum(most, size[8 * i : 8 * i + 8])
+        top[...] = jnp.maximum(top[...], most)
         n1[rows] = first.astype(jnp.bfloat16)
         n2[rows] = second.astype(jnp.bfloat16)
-        for cp in gcopies(q) + lcopies(q):
+        for cp in lcopies(q):
             cp.start()
 
-    def fcopies(q):
+        @pl.when(q < QN - 1)
+        def _():
+            for cp in gcopies(q):
+                cp.start()
+
+    def fcopies(g, last=None):
+        km, kp, ko = 2 * zm + c, 2 * zp + c, 2 * zo + c
+        lo, hi = block(km, g, last, 1), block(kp, g, last, 2)
+        bm, bp, bo = block(km, g, last), block(kp, g, last), block(ko, g, last)
         return (
-            rc(block(zm, q, 0, 64), block(zm, q, 0, 64), gs.at[q, 2], gr.at[q, 2], up),
-            rc(block(zp, q, 64, 64), block(zp, q, 64, 64), gs.at[q, 3], gr.at[q, 3], down),
-            rc(block(zm, q), block(zm, q), gs.at[q, 5], gr.at[q, 5], sib),
-            rc(block(zp, q), block(zp, q), gs.at[q, 6], gr.at[q, 6], sib),
-            rc(block(zo, q), block(zo, q), gs.at[q, 7], gr.at[q, 7], sib),
+            rc(lo, lo, gs.at[g, 2], gr.at[g, 2], up),
+            rc(hi, hi, gs.at[g, 3], gr.at[g, 3], down),
+            rc(bm, bm, gs.at[g, 5], gr.at[g, 5], sib),
+            rc(bp, bp, gs.at[g, 6], gr.at[g, 6], sib),
+            rc(bo, bo, gs.at[g, 7], gr.at[g, 7], sib),
         )
 
-    def forward_one(j):
-        q = j // 2
-        g, f = gcopies(q), fcopies(q)
-        g[0].wait_recv()
+    def forward_one(g, last=None):
+        w, f = gcopies(g, last), fcopies(g, last)
+        w[0].wait_recv()
         f[0].start()
         f[2].start()
-        g[1].wait_recv()
+        w[1].wait_recv()
         f[1].start()
         f[3].start()
 
-    def forward_two(j):
-        f = fcopies(j // 2)
-        f[0].wait_recv()
-        f[1].wait_recv()
+    def forward_two(g, last=None):
+        ko = 2 * zo + c
+        f = fcopies(g, last)
+        lo, hi = block(ko, g, last, 1), block(ko, g, last, 2)
+        rc(lo, lo, gs.at[g, 2], gr.at[g, 2], up).wait_recv()
+        rc(hi, hi, gs.at[g, 3], gr.at[g, 3], down).wait_recv()
         f[4].start()
 
     for j in range(AHEAD):
         start1(j)
+    start2(0)
+    start1(AHEAD)
 
     ins[0].wait()
     slot = lax.broadcasted_iota(jnp.int32, (64, FFN), 0)
@@ -247,6 +297,7 @@
         HT[:, pl.ds(128 * s, 128)] = jnp.concatenate(parts, axis=0).T.astype(jnp.bfloat16)
     for cp in ins[1:]:
         cp.wait()
+    top[...] = jnp.zeros_like(top)
 
     def step(t, carry):
         @pl.when(t < NC)
@@ -257,16 +308,18 @@
         def _():
             start1(t + AHEAD)
 
-        def stage(lag, fn):
+        def stage(lag, fn, last=NC):
             j = t - lag
 
-            @pl.when((j >= 0) & (j < NC) & (lax.rem(j + 2 * NC, 2) == c))
+            @pl.when((j >= 0) & (j < last) & (lax.rem(j + 2 * NC, 2) == c))
             def _():
                 fn(j)
 
-        stage(4, forward_two)
-        stage(3, forward_one)
-
+        stage(2, reduce_one)
+        stage(3, finish)
+        stage(5, lambda j: forward_two(j // 2), NC - 2)
+        stage(4, lambda j: forward_one(j // 2), NC - 2)
+        stage(2, reduce_two)
         j = t - 1
 
         @pl.when((j >= 0) & (j < NC))
@@ -277,30 +330,65 @@
             def _():
                 to_sibling(j).start()
 
-        stage(1, reduce_one)
-        stage(2, reduce_two)
-        stage(2, finish)
         return carry
 
-    lax.fori_loop(0, NC + 4, step, 0)
-
-    def drain(q, carry):
-        f = fcopies(q)
+    lax.fori_loop(1, NC + 3, step, 0)
+
+    tile = top[:, pl.ds(0, 128)]
+    for i in range(1, FFN // 128):
+        tile = jnp.maximum(tile, top[:, pl.ds(128 * i, 128)])
+    PK[k] = tile
+    pcopies = []
+    for i in range(1, 8):
+        p = lax.rem(k + i, 8)
+        pcopies.append(rc(PK.at[k], PK.at[k], ps.at[i - 1], pr.at[i - 1], (e, p)))
+        pcopies[-1].start()
+    for cp in gcopies(QN - 1, 0):
+        cp.start()
+    for cp in pcopies:
+        cp.wait_recv()
+    peak = jnp.max(PK[...])
+    pk_ref[...] = jnp.full((8, 128), peak, jnp.float32)
+    shrink, factor = scale_factors(peak, 8)
+
+    def put(start, first, n):
+        rows = nm[pl.ds(first, n)].reshape(n // 8, 8, FFN)
+        sl[pl.ds(start, n)] = ((rows * shrink) * factor).reshape(n, FFN).astype(jnp.bfloat16)
+
+    for q in range(QN - 1):
+        put(LATE * q, 128 * q + EARLY, LATE)
+    for cp in gcopies(QN, 1):
+        cp.start()
+    put(LA, 128 * (QN - 1) + EARLY_LAST, LB)
+    for cp in gcopies(QN + 1, 2):
+        cp.start()
+    for last in range(3):
+        forward_one(QN - 1 + last, last)
+    for last in range(3):
+        forward_two(QN - 1 + last, last)
+
+    def drain(g, last):
         blocks = (z, zm, zp, zo)
         for i in range(4):
-            start = (2 * blocks[i] + 1 - c) * 512 + 128 * q
-            b = w_ref.at[pl.ds(pl.multiple_of(start, 128), 128)]
-            rc(b, b, gs.at[q, 4 + i], gr.at[q, 4 + i], sib).wait_recv()
-        for cp in gcopies(q) + f:
+            b = block(2 * blocks[i] + 1 - c, g, last)
+            rc(b, b, gs.at[g, 4 + i], gr.at[g, 4 + i], sib).wait_recv()
+        w = gcopies(g, last)
+        for cp in w[:3] + fcopies(g, last):
             cp.wait_send()
+        w[3].wait()
+
+    for cp in pcopies:
+        cp.wait_send()
+    for g in range(QN - 1):
+        drain(g, None)
+    for last in range(3):
+        drain(QN - 1 + last, last)
+    for q in range(QN):
         for cp in lcopies(q):
             cp.wait()
         for cp in zcopies(2 * q + c):
             cp.wait_send()
         to_sibling(2 * q + 1 - c).wait_send()
-        return carry
-
-    lax.fori_loop(0, NC // 2, drain, 0)
 
     def drain_sends(j, carry):
         for h in (0, 1):
@@ -323,12 +411,15 @@
         exchange_kernel,
         name="exchange",
         out_shape=(
-            jax.ShapeDtypeStruct((D, FFN), f32),
+            jax.ShapeDtypeStruct((8, EN, FFN), f32),
+            jax.ShapeDtypeStruct((8, LN, FFN), bf16),
+            jax.ShapeDtypeStruct((rows, FFN), f32),
             jax.ShapeDtypeStruct((rows, FFN), bf16),
             jax.ShapeDtypeStruct((rows, FFN), bf16),
+            jax.ShapeDtypeStruct((8, 128), f32),
         ),
         in_specs=[any_spec, any_spec, pl.BlockSpec(memory_space=pltpu.SMEM), any_spec, any_spec, any_spec],
-        out_specs=(any_spec, any_spec, any_spec),
+        out_specs=(any_spec,) * 5 + (pl.BlockSpec(memory_space=pltpu.VMEM),),
         scratch_shapes=[
             V((NC, 4, 4, 64, 512), bf16),
             V((NC, 4, 4, 32, 512), bf16),
@@ -345,6 +436,9 @@
             V((rows, FFN), f32),
             V((rows, FFN), bf16),
             V((rows, FFN), bf16),
+            V((LN, FFN), bf16),
+            V((8, 8, 128), f32),
+            V((8, FFN), f32),
             DMA((2, NC)),
             DMA((2, NC, 3)),
             DMA((2, NC, 3)),
@@ -355,10 +449,13 @@
             DMA((NC // 2,)),
             DMA((NC // 2, 6)),
             DMA((NC // 2, 6)),
-            DMA((NC // 2, 8)),
-            DMA((NC // 2, 8)),
-            DMA((NC // 2, 3)),
+            DMA((QN + 2, 8)),
+            DMA((QN + 2, 8)),
+            DMA((QN + 2,)),
+            DMA((QN, 3)),
             DMA((4,)),
+            DMA((7,)),
+            DMA((7,)),
         ],
         compiler_params=pltpu.CompilerParams(
             collective_id=0, has_side_effects=True, vmem_limit_bytes=62 << 20
@@ -370,52 +467,48 @@
 ROWS = D // BLOCKS
 
 
-def scale_kernel(w_ref, m1_ref, m2_ref, nm_ref, m1o_ref, m2o_ref, s_ref, peak_ref, wv, sv, v1, v2, isem, osem):
-    k = lax.axis_index("edata")
+def scale_kernel(
+    w_ref, sl_ref, nmi_ref, m1_ref, m2_ref, pk_ref,
+    nm_ref, m1o_ref, m2o_ref, s_ref, peak_ref,
+    wv, sv, v0, v1, v2, isem, lsem, osem, ssem,
+):
     lc = pltpu.make_async_copy
+    early = [(128 * q, EARLY * q, EARLY) for q in range(QN - 1)] + [(128 * (QN - 1), EARLY * (QN - 1), EARLY_LAST)]
+    late = [(128 * q + EARLY, LATE * q, LATE) for q in range(QN - 1)] + [(128 * (QN - 1) + EARLY_LAST, LA, LB)]
 
     def load(b):
-        return lc(w_ref.at[pl.ds(b * ROWS, ROWS)], wv.at[b], isem.at[b])
+        return [lc(w_ref.at[b], wv.at[b], isem.at[b])] + [
+            lc(sl_ref.at[b, pl.ds(o, n)], sv.at[b, pl.ds(r, n)], lsem.at[b, i]) for i, (r, o, n) in enumerate(late)
+        ]
 
     for b in range(BLOCKS):
-        load(b).start()
-    small = (lc(m1_ref, v1, isem.at[BLOCKS]), lc(m2_ref, v2, isem.at[BLOCKS + 1]))
+        for cp in load(b):
+            cp.start()
+    small = (lc(nmi_ref, v0, ssem.at[0]), lc(m1_ref, v1, ssem.at[1]), lc(m2_ref, v2, ssem.at[2]))
     for cp in small:
         cp.start()
-    top = jnp.zeros((64, FFN), jnp.float32)
+    peak = jnp.max(pk_ref[...])
+    peak_ref[0] = peak
+    shrink, factor = scale_factors(peak, 8)
+    outs = []
     for b in range(BLOCKS):
-        load(b).wait()
-
-        def biggest(i, best, b=b):
-            return jnp.maximum(best, jnp.abs(wv[b, pl.ds(pl.multiple_of(64 * i, 64), 64)]))
-
-        top = lax.fori_loop(0, ROWS // 64, biggest, top)
-    outs = [lc(wv.at[k], nm_ref, osem.at[BLOCKS])]
-    outs[0].start()
-    for cp, v, o, i in ((small[0], v1, m1o_ref, 1), (small[1], v2, m2o_ref, 2)):
-        cp.wait()
+        for cp in load(b):
+            cp.wait()
+
+        for r, o, n in early:
+            v = wv[b, pl.ds(o, n)].reshape(n // 8, 8, FFN)
+            sv[b, pl.ds(r, n)] = ((v * shrink) * factor).reshape(n, FFN).astype(jnp.bfloat16)
+        outs.append(lc(sv.at[b], s_ref.at[pl.ds(b * ROWS, ROWS)], osem.at[b]))
+        outs[-1].start()
+    for i, (v, o) in enumerate(((v0, nm_ref), (v1, m1o_ref), (v2, m2o_ref))):
+        small[i].wait()
         outs.append(lc(v, o, osem.at[BLOCKS + i]))
-        outs[-1].start()
-    peak = jnp.max(top)
-    peak_ref[0] = peak
-    whole = jnp.full((8, FFN), peak + peak_eps, jnp.float32)
-    shrink = jnp.where(whole > 2.0**100, jnp.float32(2.0**-64), jnp.float32(1.0))
-    factor = 1.0 / (whole * shrink)
-    for b in range(BLOCKS):
-        def put(i, carry, b=b):
-            rows = pl.ds(pl.multiple_of(64 * i, 64), 64)
-            v = wv[b, rows].reshape(8, 8, FFN)
-            sv[b, rows] = ((v * shrink) * factor).reshape(64, FFN).astype(jnp.bfloat16)
-            return carry
-
-        lax.fori_loop(0, ROWS // 64, put, 0)
-        outs.append(lc(sv.at[b], s_ref.at[pl.ds(b * ROWS, ROWS)], osem.at[b]))
         outs[-1].start()
     for cp in outs:
         cp.wait()
 
 
-def scale(w, m1, m2):
+def scale(w, sl, nm, m1, m2, pk):
     V, DMA = pltpu.VMEM, pltpu.SemaphoreType.DMA
     f32, bf16 = jnp.float32, jnp.bfloat16
     any_spec = pl.BlockSpec(memory_space=pl.ANY)
@@ -430,24 +523,28 @@
             jax.ShapeDtypeStruct((D, FFN), bf16),
             jax.ShapeDtypeStruct((1,), f32),
         ),
-        in_specs=[any_spec] * 3,
+        in_specs=[any_spec] * 5 + [pl.BlockSpec(memory_space=pltpu.VMEM)],
         out_specs=(any_spec,) * 4 + (pl.BlockSpec(memory_space=pltpu.SMEM),),
         scratch_shapes=[
-            V((BLOCKS, ROWS, FFN), f32),
+            V((BLOCKS, EN, FFN), f32),
             V((BLOCKS, ROWS, FFN), bf16),
+            V((rows, FFN), f32),
             V((rows, FFN), bf16),
             V((rows, FFN), bf16),
-            DMA((BLOCKS + 2,)),
+            DMA((BLOCKS,)),
+            DMA((BLOCKS, QN)),
             DMA((BLOCKS + 3,)),
+            DMA((3,)),
         ],
-        compiler_params=pltpu.CompilerParams(vmem_limit_bytes=40 << 20),
-    )(w, m1, m2)
+        compiler_params=pltpu.CompilerParams(vmem_limit_bytes=63 << 20),
+    )(w, sl, nm, m1, m2, pk)
 
 
 def local(out_grad, hidden_saved, recv_counts, master_weight, moment_one, moment_two):
-    w, n1, n2 = exchange(out_grad, hidden_saved, recv_counts, master_weight, moment_one, moment_two)
-    new_master, n1, n2, scaled, peak = scale(w, n1, n2)
-    return new_master, n1, n2, scaled, peak
+    w, sl, nm, n1, n2, pk = exchange(
+        out_grad, hidden_saved, recv_counts, master_weight, moment_one, moment_two
+    )
+    return scale(w, sl, nm, n1, n2, pk)
 
 
 def solution(mesh):

time: 174 us -> 159 us (0.914)
  Pallas kernels: 166 us -> 158 us
  local copies, waits for them, and re-layouts: 6.83 us -> 0 us
    pallas_call x1, Pallas kernels: 159 us -> 148 us  [exchange(): pl.pallas_call(exchange_kernel, name='exchange', out_shape=(jax.ShapeDtyp...]
    unnamed x6 -> x0, local copies, waits for them, and re-layouts: 6.83 us -> none
    pallas_call x1, Pallas kernels: 7.41 us -> 10.1 us  [scale(): pl.pallas_call(scale_kernel, name='scale', out_shape=(jax.ShapeDtypeStruc...]
where the time goes in v2:
time: 159 us
  Pallas kernels  158 us (99%)
    pallas_call x1, Pallas kernels, exchange(): pl.pallas_call(exchange_kernel, name='exchange', out_shape=(jax.ShapeDtyp...  148 us
    pallas_call x1, Pallas kernels, scale(): pl.pallas_call(scale_kernel, name='scale', out_shape=(jax.ShapeDtypeStruc...  10.1 us

profile of v2, /device:TPU:1, one launch (start us, length us, event | category | flops | bytes accessed | tf_op | source)
XLA Modules:
  0.0 159.0 jit_solution(1567467285850293436)
XLA Ops:
  0.6 148.3 %exchange.1 = (f32[8,336,768]{2,1,0:T(8,128)}, bf16[8,176,768]{2,1,0:T(8,128)(2,1)}, f32[512,768]{1,0:T(8,128)}, bf16[512,768]{1,0:T(8,128)(2,1)}, bf16[512,768]{1,0:T(8,128)(2,1)}, /*index=5*/f32[8,128]{1,0:T(8,128)}) custom-call(bf16[4,4,64,4096]{3,2,1,0:T(8,128)(2,1)} %bitcast.1, bf16[1024,768]{1,0:T(8,128)(2,1)} %h_ref.1, s32[16]{0:T(128)} %cnt_ref.1, ...), custom_call_target="tpu_custom_call" | custom-call | tf_op jit(solution)/shard_map/exchange/pallas_call | solution.py:410
  148.9 10.1 %scale.1 = (f32[512,768]{1,0:T(8,128)}, bf16[512,768]{1,0:T(8,128)(2,1)}, bf16[512,768]{1,0:T(8,128)(2,1)}, bf16[4096,768]{1,0:T(8,128)(2,1)}, f32[1]{0:T(128)}) custom-call(f32[8,336,768]{2,1,0:T(8,128)} %get-tuple-element.11.w_ref, bf16[8,176,768]{2,1,0:T(8,128)(2,1)} %get-tuple-element.12.sl_ref, f32[512,768]{1,0:T(8,128)} %get-tuple-element.13.nmi_ref, ...), custom_call_target="tpu_custom_call" | custom-call | tf_op jit(solution)/shard_map/scale/pallas_call | solution.py:516

commit v3 on v2

--- a/solution.py
+++ b/solution.py
@@ -24,8 +24,8 @@
 NC = 8
 AHEAD = 2
 QN = NC // 2
-EARLY = 96
-EARLY_LAST = 48
+EARLY = 64
+EARLY_LAST = 64
 LATE = 128 - EARLY
 EN = (QN - 1) * EARLY + EARLY_LAST
 LN = 128 * QN - EN
@@ -317,9 +317,6 @@
 
         stage(2, reduce_one)
         stage(3, finish)
-        stage(5, lambda j: forward_two(j // 2), NC - 2)
-        stage(4, lambda j: forward_one(j // 2), NC - 2)
-        stage(2, reduce_two)
         j = t - 1
 
         @pl.when((j >= 0) & (j < NC))
@@ -330,6 +327,9 @@
             def _():
                 to_sibling(j).start()
 
+        stage(2, reduce_two)
+        stage(5, lambda j: forward_two(j // 2), NC - 2)
+        stage(4, lambda j: forward_one(j // 2), NC - 2)
         return carry
 
     lax.fori_loop(1, NC + 3, step, 0)
@@ -481,16 +481,20 @@
             lc(sl_ref.at[b, pl.ds(o, n)], sv.at[b, pl.ds(r, n)], lsem.at[b, i]) for i, (r, o, n) in enumerate(late)
         ]
 
+    small = (lc(nmi_ref, v0, ssem.at[0]), lc(m1_ref, v1, ssem.at[1]), lc(m2_ref, v2, ssem.at[2]))
+    for cp in small:
+        cp.start()
     for b in range(BLOCKS):
         for cp in load(b):
             cp.start()
-    small = (lc(nmi_ref, v0, ssem.at[0]), lc(m1_ref, v1, ssem.at[1]), lc(m2_ref, v2, ssem.at[2]))
-    for cp in small:
-        cp.start()
     peak = jnp.max(pk_ref[...])
     peak_ref[0] = peak
     shrink, factor = scale_factors(peak, 8)
     outs = []
+    for i, (v, o) in enumerate(((v0, nm_ref), (v1, m1o_ref), (v2, m2o_ref))):
+        small[i].wait()
+        outs.append(lc(v, o, osem.at[BLOCKS + i]))
+        outs[-1].start()
     for b in range(BLOCKS):
         for cp in load(b):
             cp.wait()
@@ -499,10 +503,6 @@
             v = wv[b, pl.ds(o, n)].reshape(n // 8, 8, FFN)
             sv[b, pl.ds(r, n)] = ((v * shrink) * factor).reshape(n, FFN).astype(jnp.bfloat16)
         outs.append(lc(sv.at[b], s_ref.at[pl.ds(b * ROWS, ROWS)], osem.at[b]))
-        outs[-1].start()
-    for i, (v, o) in enumerate(((v0, nm_ref), (v1, m1o_ref), (v2, m2o_ref))):
-        small[i].wait()
-        outs.append(lc(v, o, osem.at[BLOCKS + i]))
         outs[-1].start()
     for cp in outs:
         cp.wait()

time: 159 us -> 156 us (0.981)
  Pallas kernels: 158 us -> 156 us
    pallas_call x1, Pallas kernels: 148 us -> 147 us  [exchange(): pl.pallas_call(exchange_kernel, name='exchange', out_shape=(jax.ShapeDtyp...]
where the time goes in v3:
time: 156 us
  Pallas kernels  156 us (100%)
    pallas_call x1, Pallas kernels, exchange(): pl.pallas_call(exchange_kernel, name='exchange', out_shape=(jax.ShapeDtyp...  147 us
    pallas_call x1, Pallas kernels, scale(): pl.pallas_call(scale_kernel, name='scale', out_shape=(jax.ShapeDtypeStruc...  8.97 us

profile of v3, /device:TPU:1, one launch (start us, length us, event | category | flops | bytes accessed | tf_op | source)
XLA Modules:
  0.0 156.2 jit_solution(237039183722848838)
XLA Ops:
  0.6 146.6 %exchange.1 = (f32[8,256,768]{2,1,0:T(8,128)}, bf16[8,256,768]{2,1,0:T(8,128)(2,1)}, f32[512,768]{1,0:T(8,128)}, bf16[512,768]{1,0:T(8,128)(2,1)}, bf16[512,768]{1,0:T(8,128)(2,1)}, /*index=5*/f32[8,128]{1,0:T(8,128)}) custom-call(bf16[4,4,64,4096]{3,2,1,0:T(8,128)(2,1)} %bitcast.1, bf16[1024,768]{1,0:T(8,128)(2,1)} %h_ref.1, s32[16]{0:T(128)} %cnt_ref.1, ...), custom_call_target="tpu_custom_call" | custom-call | tf_op jit(solution)/shard_map/exchange/pallas_call | solution.py:410
  147.2 9.0 %scale.1 = (f32[512,768]{1,0:T(8,128)}, bf16[512,768]{1,0:T(8,128)(2,1)}, bf16[512,768]{1,0:T(8,128)(2,1)}, bf16[4096,768]{1,0:T(8,128)(2,1)}, f32[1]{0:T(128)}) custom-call(f32[8,256,768]{2,1,0:T(8,128)} %get-tuple-element.11.w_ref, bf16[8,256,768]{2,1,0:T(8,128)(2,1)} %get-tuple-element.12.sl_ref, f32[512,768]{1,0:T(8,128)} %get-tuple-element.13.nmi_ref, ...), custom_call_target="tpu_custom_call" | custom-call | tf_op jit(solution)/shard_map/scale/pallas_call | solution.py:516

commit v4 on v3

--- a/solution.py
+++ b/solution.py
@@ -24,12 +24,13 @@
 NC = 8
 AHEAD = 2
 QN = NC // 2
-EARLY = 64
-EARLY_LAST = 64
+QF = 2
+EARLY = 112
+EARLY_LAST = 32
 LATE = 128 - EARLY
-EN = (QN - 1) * EARLY + EARLY_LAST
+EN = QF * EARLY + EARLY_LAST
 LN = 128 * QN - EN
-LA = (QN - 1) * LATE
+LA = QF * LATE + (QN - 1 - QF) * 128
 LB = 128 - EARLY_LAST
 
 
@@ -192,7 +193,7 @@
         if last is None:
             return w_ref, pl.multiple_of(EARLY * g, 8), EARLY, EARLY // 2
         return (
-            (w_ref, (QN - 1) * EARLY, EARLY_LAST, EARLY_LAST // 2),
+            (w_ref, QF * EARLY, EARLY_LAST, EARLY_LAST // 2),
             (sl_ref, 0, LA, LA // 32 * 16),
             (sl_ref, LA, LB, (LB + 31) // 32 * 16),
         )[last]
@@ -248,7 +249,7 @@
         for cp in lcopies(q):
             cp.start()
 
-        @pl.when(q < QN - 1)
+        @pl.when(q < QF)
         def _():
             for cp in gcopies(q):
                 cp.start()
@@ -328,8 +329,8 @@
                 to_sibling(j).start()
 
         stage(2, reduce_two)
-        stage(5, lambda j: forward_two(j // 2), NC - 2)
-        stage(4, lambda j: forward_one(j // 2), NC - 2)
+        stage(5, lambda j: forward_two(j // 2), 2 * QF)
+        stage(4, lambda j: forward_one(j // 2), 2 * QF)
         return carry
 
     lax.fori_loop(1, NC + 3, step, 0)
@@ -343,7 +344,7 @@
         p = lax.rem(k + i, 8)
         pcopies.append(rc(PK.at[k], PK.at[k], ps.at[i - 1], pr.at[i - 1], (e, p)))
         pcopies[-1].start()
-    for cp in gcopies(QN - 1, 0):
+    for cp in gcopies(QF, 0):
         cp.start()
     for cp in pcopies:
         cp.wait_recv()
@@ -355,17 +356,19 @@
         rows = nm[pl.ds(first, n)].reshape(n // 8, 8, FFN)
         sl[pl.ds(start, n)] = ((rows * shrink) * factor).reshape(n, FFN).astype(jnp.bfloat16)
 
-    for q in range(QN - 1):
+    for q in range(QF):
         put(LATE * q, 128 * q + EARLY, LATE)
-    for cp in gcopies(QN, 1):
+    for q in range(QF, QN - 1):
+        put(LATE * QF + 128 * (q - QF), 128 * q, 128)
+    for cp in gcopies(QF + 1, 1):
         cp.start()
     put(LA, 128 * (QN - 1) + EARLY_LAST, LB)
-    for cp in gcopies(QN + 1, 2):
+    for cp in gcopies(QF + 2, 2):
         cp.start()
     for last in range(3):
-        forward_one(QN - 1 + last, last)
+        forward_one(QF + last, last)
     for last in range(3):
-        forward_two(QN - 1 + last, last)
+        forward_two(QF + last, last)
 
     def drain(g, last):
         blocks = (z, zm, zp, zo)
@@ -379,10 +382,10 @@
 
     for cp in pcopies:
         cp.wait_send()
-    for g in range(QN - 1):
+    for g in range(QF):
         drain(g, None)
     for last in range(3):
-        drain(QN - 1 + last, last)
+        drain(QF + last, last)
     for q in range(QN):
         for cp in lcopies(q):
             cp.wait()
@@ -473,8 +476,10 @@
     wv, sv, v0, v1, v2, isem, lsem, osem, ssem,
 ):
     lc = pltpu.make_async_copy
-    early = [(128 * q, EARLY * q, EARLY) for q in range(QN - 1)] + [(128 * (QN - 1), EARLY * (QN - 1), EARLY_LAST)]
-    late = [(128 * q + EARLY, LATE * q, LATE) for q in range(QN - 1)] + [(128 * (QN - 1) + EARLY_LAST, LA, LB)]
+    early = [(128 * q, EARLY * q, EARLY) for q in range(QF)] + [(128 * (QN - 1), EARLY * QF, EARLY_LAST)]
+    late = [(128 * q + EARLY, LATE * q, LATE) for q in range(QF)] + [
+        (128 * q, LATE * QF + 128 * (q - QF), 128) for q in range(QF, QN - 1)
+    ] + [(128 * (QN - 1) + EARLY_LAST, LA, LB)]
 
     def load(b):
         return [lc(w_ref.at[b], wv.at[b], isem.at[b])] + [

time: 156 us -> 153 us (0.981)
  Pallas kernels: 156 us -> 152 us
    pallas_call x1, Pallas kernels: 147 us -> 143 us  [exchange(): pl.pallas_call(exchange_kernel, name='exchange', out_shape=(jax.ShapeDtyp...]
where the time goes in v4:
time: 153 us
  Pallas kernels  152 us (99%)
    pallas_call x1, Pallas kernels, exchange(): pl.pallas_call(exchange_kernel, name='exchange', out_shape=(jax.ShapeDtyp...  143 us
    pallas_call x1, Pallas kernels, scale(): pl.pallas_call(scale_kernel, name='scale', out_shape=(jax.ShapeDtypeStruc...  8.98 us

profile of v4, /device:TPU:1, one launch (start us, length us, event | category | flops | bytes accessed | tf_op | source)
XLA Modules:
  0.0 152.6 jit_solution(3970900029871797681)
XLA Ops:
  0.6 142.9 %exchange.1 = (f32[8,256,768]{2,1,0:T(8,128)}, bf16[8,256,768]{2,1,0:T(8,128)(2,1)}, f32[512,768]{1,0:T(8,128)}, bf16[512,768]{1,0:T(8,128)(2,1)}, bf16[512,768]{1,0:T(8,128)(2,1)}, /*index=5*/f32[8,128]{1,0:T(8,128)}) custom-call(bf16[4,4,64,4096]{3,2,1,0:T(8,128)(2,1)} %bitcast.1, bf16[1024,768]{1,0:T(8,128)(2,1)} %h_ref.1, s32[16]{0:T(128)} %cnt_ref.1, ...), custom_call_target="tpu_custom_call" | custom-call | tf_op jit(solution)/shard_map/exchange/pallas_call | solution.py:413
  143.6 9.0 %scale.1 = (f32[512,768]{1,0:T(8,128)}, bf16[512,768]{1,0:T(8,128)(2,1)}, bf16[512,768]{1,0:T(8,128)(2,1)}, bf16[4096,768]{1,0:T(8,128)(2,1)}, f32[1]{0:T(128)}) custom-call(f32[8,256,768]{2,1,0:T(8,128)} %get-tuple-element.11.w_ref, bf16[8,256,768]{2,1,0:T(8,128)(2,1)} %get-tuple-element.12.sl_ref, f32[512,768]{1,0:T(8,128)} %get-tuple-element.13.nmi_ref, ...), custom_call_target="tpu_custom_call" | custom-call | tf_op jit(solution)/shard_map/scale/pallas_call | solution.py:521

commit v5 on v4

--- a/solution.py
+++ b/solution.py
@@ -26,7 +26,7 @@
 QN = NC // 2
 QF = 2
 EARLY = 112
-EARLY_LAST = 32
+EARLY_LAST = 64
 LATE = 128 - EARLY
 EN = QF * EARLY + EARLY_LAST
 LN = 128 * QN - EN

time: 153 us -> 152 us (level)
  no operation moved by 1% of the time
where the time goes in v5:
time: 152 us
  Pallas kernels  151 us (99%)
    pallas_call x1, Pallas kernels, exchange(): pl.pallas_call(exchange_kernel, name='exchange', out_shape=(jax.ShapeDtyp...  142 us
    pallas_call x1, Pallas kernels, scale(): pl.pallas_call(scale_kernel, name='scale', out_shape=(jax.ShapeDtypeStruc...  9.06 us

profile of v5, /device:TPU:1, one launch (start us, length us, event | category | flops | bytes accessed | tf_op | source)
XLA Modules:
  0.0 152.0 jit_solution(15023791345832055225)
XLA Ops:
  0.6 142.3 %exchange.1 = (f32[8,288,768]{2,1,0:T(8,128)}, bf16[8,224,768]{2,1,0:T(8,128)(2,1)}, f32[512,768]{1,0:T(8,128)}, bf16[512,768]{1,0:T(8,128)(2,1)}, bf16[512,768]{1,0:T(8,128)(2,1)}, /*index=5*/f32[8,128]{1,0:T(8,128)}) custom-call(bf16[4,4,64,4096]{3,2,1,0:T(8,128)(2,1)} %bitcast.1, bf16[1024,768]{1,0:T(8,128)(2,1)} %h_ref.1, s32[16]{0:T(128)} %cnt_ref.1, ...), custom_call_target="tpu_custom_call" | custom-call | tf_op jit(solution)/shard_map/exchange/pallas_call | solution.py:413
  143.0 9.1 %scale.1 = (f32[512,768]{1,0:T(8,128)}, bf16[512,768]{1,0:T(8,128)(2,1)}, bf16[512,768]{1,0:T(8,128)(2,1)}, bf16[4096,768]{1,0:T(8,128)(2,1)}, f32[1]{0:T(128)}) custom-call(f32[8,288,768]{2,1,0:T(8,128)} %get-tuple-element.11.w_ref, bf16[8,224,768]{2,1,0:T(8,128)(2,1)} %get-tuple-element.12.sl_ref, f32[512,768]{1,0:T(8,128)} %get-tuple-element.13.nmi_ref, ...), custom_call_target="tpu_custom_call" | custom-call | tf_op jit(solution)/shard_map/scale/pallas_call | solution.py:521

commit v6 on v5

--- a/solution.py
+++ b/solution.py
@@ -26,7 +26,7 @@
 QN = NC // 2
 QF = 2
 EARLY = 112
-EARLY_LAST = 64
+EARLY_LAST = 80
 LATE = 128 - EARLY
 EN = QF * EARLY + EARLY_LAST
 LN = 128 * QN - EN
@@ -239,6 +239,12 @@
         weight = mw[rows]
         weight = weight - learn_rate * (update + weight_decay * weight)
         nm[rows] = weight
+
+        @pl.when(q < QF)
+        def _():
+            for cp in gcopies(q):
+                cp.start()
+
         size = jnp.abs(weight)
         most = size[:8]
         for i in range(1, 16):
@@ -248,11 +254,6 @@
         n2[rows] = second.astype(jnp.bfloat16)
         for cp in lcopies(q):
             cp.start()
-
-        @pl.when(q < QF)
-        def _():
-            for cp in gcopies(q):
-                cp.start()
 
     def fcopies(g, last=None):
         km, kp, ko = 2 * zm + c, 2 * zp + c, 2 * zo + c

time: 152 us -> 153 us (level)
  no operation moved by 1% of the time
where the time goes in v6:
time: 153 us; the launch traced here: 152 us
  Pallas kernels  152 us (99%)
    pallas_call x1, Pallas kernels, exchange(): pl.pallas_call(exchange_kernel, name='exchange', out_shape=(jax.ShapeDtyp...  143 us
    pallas_call x1, Pallas kernels, scale(): pl.pallas_call(scale_kernel, name='scale', out_shape=(jax.ShapeDtypeStruc...  9.19 us

profile of v6, /device:TPU:1, one launch (start us, length us, event | category | flops | bytes accessed | tf_op | source)
XLA Modules:
  0.0 152.4 jit_solution(9367023633336923930)
XLA Ops:
  0.6 142.6 %exchange.1 = (f32[8,304,768]{2,1,0:T(8,128)}, bf16[8,208,768]{2,1,0:T(8,128)(2,1)}, f32[512,768]{1,0:T(8,128)}, bf16[512,768]{1,0:T(8,128)(2,1)}, bf16[512,768]{1,0:T(8,128)(2,1)}, /*index=5*/f32[8,128]{1,0:T(8,128)}) custom-call(bf16[4,4,64,4096]{3,2,1,0:T(8,128)(2,1)} %bitcast.1, bf16[1024,768]{1,0:T(8,128)(2,1)} %h_ref.1, s32[16]{0:T(128)} %cnt_ref.1, ...), custom_call_target="tpu_custom_call" | custom-call | tf_op jit(solution)/shard_map/exchange/pallas_call | solution.py:414
  143.2 9.2 %scale.1 = (f32[512,768]{1,0:T(8,128)}, bf16[512,768]{1,0:T(8,128)(2,1)}, bf16[512,768]{1,0:T(8,128)(2,1)}, bf16[4096,768]{1,0:T(8,128)(2,1)}, f32[1]{0:T(128)}) custom-call(f32[8,304,768]{2,1,0:T(8,128)} %get-tuple-element.11.w_ref, bf16[8,208,768]{2,1,0:T(8,128)(2,1)} %get-tuple-element.12.sl_ref, f32[512,768]{1,0:T(8,128)} %get-tuple-element.13.nmi_ref, ...), custom_call_target="tpu_custom_call" | custom-call | tf_op jit(solution)/shard_map/scale/pallas_call | solution.py:522
